TPU v7x, 32 devices: a whole 2x2x4 slice. The times are simulated.
32 devices in a mesh: rep: 2 (over core), fsdp: 16 (over z, y, x).
Axes of the slice: x: 2, y: 2, z: 4, core: 2. Of those that a mesh axis runs over, the one named last changes fastest.
Arguments:
- tokens: bfloat16 [16384, 768], P(('rep', 'fsdp')), may hold values from -6 to 6
- valid: int32 [128], P(('rep', 'fsdp')), may hold values from 1 to 192, as said below
- qkv_weight: float32 [2, 768, 2304], P(None, 'fsdp'), may hold values from -0.3125 to 0.3125
- out_weight: float32 [2, 768, 768], P(None, 'fsdp'), may hold values from -0.875 to 0.875
- up_weight: float32 [2, 768, 3072], P(None, 'fsdp'), may hold values from -0.21875 to 0.21875
- down_weight: float32 [2, 3072, 768], P(None, 'fsdp'), may hold values from -0.109375 to 0.109375
- vectors: float32 [2, 9216], P(None, 'fsdp'), may hold values from -0.9 to 1.6, as said below
- cotangent: bfloat16 [16384, 768], P(('rep', 'fsdp')), may hold values from -6 to 6
Outputs:
- layer_out: bfloat16 [16384, 768], P(('rep', 'fsdp'))
- input_grad: float32 [16384, 768], P(('rep', 'fsdp'))
- qkv_grad: float32 [2, 768, 2304], P(None, 'fsdp')
- out_grad: float32 [2, 768, 768], P(None, 'fsdp')
- up_grad: float32 [2, 768, 3072], P(None, 'fsdp')
- down_grad: float32 [2, 3072, 768], P(None, 'fsdp')
- vector_grad: float32 [2, 9216], P(None, 'fsdp')
Inputs may be any that keep to these rules, and one draw needn't show every extreme that they name: `valid`: pair p sits in slot p mod 4 of its group; a pair of a slot of k * 64 rows has more than (k - 1) * 64 real rows; pair 0 fills its slot. `vectors`: norm gains lie between 0.4 and 1.6, the biases between -0.9 and 0.9.
All inputs are finite; a program needn't handle non-finite values.
Results may differ from a plain program's by a relative error of at most 0.029.
The roundings to bfloat16 on the way count: a program that leaves them out, or rounds other values in their place, can miss the bound.
Values may be sent and summed in bfloat16 or wider, within the bound.
No kernel may reach another device: no remote copies, remote signals or barrier semaphores. Data moves between devices by JAX's collectives and lax.ppermute only.
A program may use at most 192 MiB of HBM per device.

v0:
```python
import jax
import jax.numpy as jnp
from jax import lax
from jax.sharding import PartitionSpec as P

HEADS = 12
HD = 64
LAYERS = 2
LEN_UNIT = 64
NORM_EPSILON = 1e-05
NEG_LARGE = -1e30
SCORE_SCALE = 0.125


def slot_layout(valid_groups):
    row_index = jnp.arange(8 * LEN_UNIT, dtype=jnp.int32)
    slot_index = (
        (row_index >= 3 * LEN_UNIT).astype(jnp.int32)
        + (row_index >= 5 * LEN_UNIT).astype(jnp.int32)
        + (row_index >= 7 * LEN_UNIT).astype(jnp.int32)
    )
    slot_start = jnp.where(
        slot_index == 0,
        0,
        jnp.where(
            slot_index == 1, 3 * LEN_UNIT, jnp.where(slot_index == 2, 5 * LEN_UNIT, 7 * LEN_UNIT)
        ),
    ).astype(jnp.int32)
    offset = row_index - slot_start
    slot_pick = (slot_index[:, None] == jnp.arange(4, dtype=jnp.int32)[None, :]).astype(jnp.int32)
    limits = jnp.sum(valid_groups[:, None, :] * slot_pick[None], -1)
    row_live = offset[None, :] < limits
    same_slot = slot_index[:, None] == slot_index[None, :]
    permitted = same_slot[None] & row_live[:, None, :]
    return (row_live, permitted)


def normed(values_in, gain_ln, bias_ln):
    row_mean = jnp.mean(values_in, -1, keepdims=True)
    centred = values_in - row_mean
    row_var = jnp.mean(centred * centred, -1, keepdims=True)
    return centred * lax.rsqrt(row_var + NORM_EPSILON) * gain_ln + bias_ln


def exact_gelu(values_in):
    return jax.nn.gelu(values_in, approximate=False)


def outer_sum(left, right):
    return lax.dot_general(
        left, right, (((0,), (0,)), ((), ())), preferred_element_type=jnp.float32
    )


def times_transposed(left, right):
    return lax.dot_general(
        left, right, (((1,), (1,)), ((), ())), preferred_element_type=jnp.float32
    )


def split_heads(qkv_low, permitted):
    group_count = permitted.shape[0]
    group_rows = permitted.shape[1]
    split_qkv = qkv_low.reshape(group_count, group_rows, 3, HEADS, HD)
    return (split_qkv[:, :, 0], split_qkv[:, :, 1], split_qkv[:, :, 2])


def raw_scores(queries, key_rows, permitted):
    scores = (
        jnp.einsum("gqhd,gkhd->ghqk", queries, key_rows, preferred_element_type=jnp.float32)
        * SCORE_SCALE
    )
    return jnp.where(permitted[:, None], scores, NEG_LARGE)


def attend(qkv_low, permitted):
    queries, key_rows, value_rows = split_heads(qkv_low, permitted)
    scores = raw_scores(queries, key_rows, permitted)
    row_top = jnp.max(scores, -1, keepdims=True)
    row_total = jnp.sum(jnp.exp(scores - row_top), -1, keepdims=True)
    log_total = row_top + jnp.log(row_total)
    probs = jnp.exp(scores - log_total).astype(jnp.bfloat16)
    context = jnp.einsum("ghqk,gkhd->gqhd", probs, value_rows, preferred_element_type=jnp.float32)
    return (context.reshape(qkv_low.shape[0], HEADS * HD).astype(jnp.bfloat16), log_total)


def attend_back(qkv_low, log_total, d_context, permitted):
    queries, key_rows, value_rows = split_heads(qkv_low, permitted)
    scores = raw_scores(queries, key_rows, permitted)
    probs = jnp.exp(scores - log_total)
    probs_low = probs.astype(jnp.bfloat16)
    d_heads = d_context.reshape(queries.shape)
    d_value = jnp.einsum("ghqk,gqhd->gkhd", probs_low, d_heads, preferred_element_type=jnp.float32)
    d_probs = jnp.einsum("gqhd,gkhd->ghqk", d_heads, value_rows, preferred_element_type=jnp.float32)
    d_scores = probs * (d_probs - jnp.sum(probs * d_probs, -1, keepdims=True))
    d_low = d_scores.astype(jnp.bfloat16)
    d_query = (
        jnp.einsum("ghqk,gkhd->gqhd", d_low, key_rows, preferred_element_type=jnp.float32)
        * SCORE_SCALE
    )
    d_key = (
        jnp.einsum("ghqk,gqhd->gkhd", d_low, queries, preferred_element_type=jnp.float32)
        * SCORE_SCALE
    )
    joined = jnp.stack([d_query, d_key, d_value], 2)
    return joined.reshape(qkv_low.shape[0], 3 * HEADS * HD)


def unpack(vector_row, model_width):
    pieces = [
        vector_row[segment * model_width : (segment + 1) * model_width] for segment in range(8)
    ]
    return (pieces, vector_row[8 * model_width :])


def forward_layer(hidden, weights, vector_row, permitted):
    w_qkv, w_out, w_up, w_down = weights
    model_width = hidden.shape[1]
    pieces, bias_u = unpack(vector_row, model_width)
    bias_q, bias_v, bias_o, gain_a, shift_a, bias_d, gain_b, shift_b = pieces
    h_low = hidden.astype(jnp.bfloat16)
    qkv_full = jnp.dot(h_low, w_qkv, preferred_element_type=jnp.float32) + jnp.concatenate(
        [bias_q, jnp.zeros_like(bias_q), bias_v]
    )
    qkv_low = qkv_full.astype(jnp.bfloat16)
    context, log_total = attend(qkv_low, permitted)
    mixed_a = jnp.dot(context, w_out, preferred_element_type=jnp.float32) + bias_o
    first_sum = hidden + mixed_a
    first = normed(first_sum, gain_a, shift_a)
    first_low = first.astype(jnp.bfloat16)
    inner = jnp.dot(first_low, w_up, preferred_element_type=jnp.float32) + bias_u
    active = exact_gelu(inner).astype(jnp.bfloat16)
    mixed_b = jnp.dot(active, w_down, preferred_element_type=jnp.float32) + bias_d
    second_sum = first + mixed_b
    second = normed(second_sum, gain_b, shift_b)
    saved = (h_low, qkv_low, log_total, context, first_sum, first_low, inner, active, second_sum)
    return (second, saved)


def backward_layer(d_out, saved, weights, vector_row, permitted):
    w_qkv, w_out, w_up, w_down = weights
    h_low, qkv_low, log_total, context, first_sum, first_low, inner, active, second_sum = saved
    model_width = h_low.shape[1]
    pieces, bias_u = unpack(vector_row, model_width)
    bias_q, bias_v, bias_o, gain_a, shift_a, bias_d, gain_b, shift_b = pieces
    unused_b, norm_b_back = jax.vjp(normed, second_sum, gain_b, shift_b)
    d_second_sum, d_gain_b, d_shift_b = norm_b_back(d_out)
    d_mixed_b = d_second_sum.astype(jnp.bfloat16)
    d_bias_d = jnp.sum(d_mixed_b, 0, dtype=jnp.float32)
    grad_down = outer_sum(active, d_mixed_b)
    d_active = times_transposed(d_mixed_b, w_down)
    unused_g, gelu_back = jax.vjp(exact_gelu, inner)
    d_inner = gelu_back(d_active)[0].astype(jnp.bfloat16)
    d_bias_u = jnp.sum(d_inner, 0, dtype=jnp.float32)
    grad_up = outer_sum(first_low, d_inner)
    d_first = d_second_sum + times_transposed(d_inner, w_up)
    unused_a, norm_a_back = jax.vjp(normed, first_sum, gain_a, shift_a)
    d_first_sum, d_gain_a, d_shift_a = norm_a_back(d_first)
    d_mixed_a = d_first_sum.astype(jnp.bfloat16)
    d_bias_o = jnp.sum(d_mixed_a, 0, dtype=jnp.float32)
    grad_out = outer_sum(context, d_mixed_a)
    d_context = times_transposed(d_mixed_a, w_out).astype(jnp.bfloat16)
    d_qkv = attend_back(qkv_low, log_total, d_context, permitted).astype(jnp.bfloat16)
    d_bias_qkv = jnp.sum(d_qkv, 0, dtype=jnp.float32)
    grad_qkv = outer_sum(h_low, d_qkv)
    d_hidden = d_first_sum + times_transposed(d_qkv, w_qkv)
    d_vector = jnp.concatenate(
        [
            d_bias_qkv[:model_width],
            d_bias_qkv[2 * model_width :],
            d_bias_o,
            d_gain_a,
            d_shift_a,
            d_bias_d,
            d_gain_b,
            d_shift_b,
            d_bias_u,
        ]
    )
    return (d_hidden, (grad_qkv, grad_out, grad_up, grad_down, d_vector))


def shards(tokens, valid, qkv_weight, out_weight, up_weight, down_weight, vectors, cotangent):
    group_count = valid.shape[0] // 4
    row_live, permitted = slot_layout(valid.reshape(group_count, 4))
    row_mask = row_live.reshape(-1, 1).astype(jnp.float32)
    vector_all = lax.all_gather(vectors, "fsdp", axis=1, tiled=True)
    hidden = tokens.astype(jnp.float32)
    kept_weights = []
    kept_saved = []
    for level_idx in range(LAYERS):
        weights = (
            lax.all_gather(qkv_weight[level_idx].astype(jnp.bfloat16), "fsdp", axis=0, tiled=True),
            lax.all_gather(out_weight[level_idx].astype(jnp.bfloat16), "fsdp", axis=0, tiled=True),
            lax.all_gather(up_weight[level_idx].astype(jnp.bfloat16), "fsdp", axis=0, tiled=True),
            lax.all_gather(down_weight[level_idx].astype(jnp.bfloat16), "fsdp", axis=0, tiled=True),
        )
        hidden, saved = forward_layer(hidden, weights, vector_all[level_idx], permitted)
        kept_weights.append(weights)
        kept_saved.append(saved)
    layer_out = (hidden * row_mask).astype(jnp.bfloat16)
    d_hidden = cotangent.astype(jnp.float32) * row_mask
    results = [None] * LAYERS
    for level_idx in reversed(range(LAYERS)):
        weights = (
            lax.all_gather(qkv_weight[level_idx].astype(jnp.bfloat16), "fsdp", axis=0, tiled=True),
            lax.all_gather(out_weight[level_idx].astype(jnp.bfloat16), "fsdp", axis=0, tiled=True),
            lax.all_gather(up_weight[level_idx].astype(jnp.bfloat16), "fsdp", axis=0, tiled=True),
            lax.all_gather(down_weight[level_idx].astype(jnp.bfloat16), "fsdp", axis=0, tiled=True),
        )
        d_hidden, terms = backward_layer(
            d_hidden, kept_saved[level_idx], weights, vector_all[level_idx], permitted
        )
        term_qkv, term_out, term_up, term_down, term_vector = terms
        owned = (
            lax.psum_scatter(
                term_qkv.astype(jnp.bfloat16), "fsdp", scatter_dimension=0, tiled=True
            ).astype(jnp.float32),
            lax.psum_scatter(
                term_out.astype(jnp.bfloat16), "fsdp", scatter_dimension=0, tiled=True
            ).astype(jnp.float32),
            lax.psum_scatter(
                term_up.astype(jnp.bfloat16), "fsdp", scatter_dimension=0, tiled=True
            ).astype(jnp.float32),
            lax.psum_scatter(
                term_down.astype(jnp.bfloat16), "fsdp", scatter_dimension=0, tiled=True
            ).astype(jnp.float32),
            lax.psum_scatter(
                term_vector.astype(jnp.bfloat16), "fsdp", scatter_dimension=0, tiled=True
            ).astype(jnp.float32),
        )
        shares = (
            lax.psum(owned[0].astype(jnp.bfloat16), "rep").astype(jnp.float32),
            lax.psum(owned[1].astype(jnp.bfloat16), "rep").astype(jnp.float32),
            lax.psum(owned[2].astype(jnp.bfloat16), "rep").astype(jnp.float32),
            lax.psum(owned[3].astype(jnp.bfloat16), "rep").astype(jnp.float32),
            lax.psum(owned[4].astype(jnp.bfloat16), "rep").astype(jnp.float32),
        )
        results[level_idx] = shares
    qkv_grad = jnp.stack([entry[0] for entry in results])
    out_grad = jnp.stack([entry[1] for entry in results])
    up_grad = jnp.stack([entry[2] for entry in results])
    down_grad = jnp.stack([entry[3] for entry in results])
    vector_grad = jnp.stack([entry[4] for entry in results])
    return (layer_out, d_hidden, qkv_grad, out_grad, up_grad, down_grad, vector_grad)


def solution(mesh):
    in_specs = (
        P(("rep", "fsdp"), None),
        P(("rep", "fsdp")),
        P(None, "fsdp", None),
        P(None, "fsdp", None),
        P(None, "fsdp", None),
        P(None, "fsdp", None),
        P(None, "fsdp"),
        P(("rep", "fsdp"), None),
    )
    out_specs = (
        P(("rep", "fsdp"), None),
        P(("rep", "fsdp"), None),
        P(None, "fsdp", None),
        P(None, "fsdp", None),
        P(None, "fsdp", None),
        P(None, "fsdp", None),
        P(None, "fsdp"),
    )
    return jax.shard_map(shards, mesh=mesh, in_specs=in_specs, out_specs=out_specs, check_vma=False)
```

profile of v0, /device:TPU:0, one launch (start us, length us, event | category | flops | bytes accessed | tf_op | source)
XLA Modules:
  0.0 1876.1 jit_solution(6135757692193599547)
XLA Ops:
  15.9 43.3 %all-gather.8 = f32[16,576,2]{1,2,0:T(2,128)S(1)} all-gather(f32[1,576,2]{1,2,0:T(2,128)S(1)} %bitcast.257), channel_id=1, replica_groups=mesh['rep'=2,'fsdp'=16] {'fsdp'}, dimensions={0}, use_global_device_ids=true | all-gather | bytes 78336 | tf_op jit(solution)/shard_map/all_gather | solution.py:187
  59.9 25.6 %all-gather.18.cloned.1.call-done = bf16[1,768,2304]{2,1,0:T(8,128)(2,1)} async-done(((bf16[1,48,2304]{2,1,0:T(8,128)(2,1)}), bf16[1,768,2304]{2,1,0:T(8,128)(2,1)}) %all-gather.18.cloned.1.call-update) | async-done | bytes 3538960 | tf_op jit(solution)/shard_map/all_gather | solution.py:193
  85.5 5.4 fusion.32
  91.0 3.0 copy.67
  94.0 2.1 fusion
  96.1 2.6 exponential_reduce_fusion.1
  98.7 2.0 copy-done
  101.3 3.9 convolution_convert_fusion.11
  105.2 38.4 %all-gather.20.cloned.1.call-done = bf16[1,768,768]{2,1,0:T(8,128)(2,1)} async-done(((bf16[1,48,768]{2,1,0:T(8,128)(2,1)}), bf16[1,768,768]{2,1,0:T(8,128)(2,1)}) %all-gather.20.cloned.1.call-update) | async-done | bytes 1179664 | tf_op jit(solution)/shard_map/all_gather | solution.py:194
  143.6 2.4 fusion.114
  146.4 80.0 %all-gather.22.cloned.1.call-done = bf16[1,768,3072]{2,1,0:T(8,128)(2,1)} async-done(((bf16[1,48,3072]{2,1,0:T(8,128)(2,1)}), bf16[1,768,3072]{2,1,0:T(8,128)(2,1)}) %all-gather.22.cloned.1.call-update) | async-done | bytes 4718608 | tf_op jit(solution)/shard_map/all_gather | solution.py:195
  226.4 20.0 %multiply_convert_fusion.3 = (bf16[512,3072]{1,0:T(8,128)(2,1)}, f32[512,3072]{1,0:T(8,128)}, f32[512,3072]{1,0:T(8,128)}) fusion(f32[3072]{0:T(1024)S(1)} %bitcast.253, bf16[1,768,3072]{2,1,0:T(8,128)(2,1)} %all-gather.22.cloned.1.call-done, f32[512,768]{1,0:T(8,128)S(1)} %get-tuple-element.107, f32[768]{0:T(1024)S(1)} %get-tuple-element.44, ...), kind=kOutput, calls=%fused_computation.33 | convolution fusion | flops 2521694208 | bytes 22042624 | tf_op jit(solution)/shard_map/dot_general | solution.py:131
  246.4 62.3 %all-gather.24.cloned.1.call-done = bf16[1,3072,768]{2,1,0:T(8,128)(2,1)} async-done(((bf16[1,192,768]{2,1,0:T(8,128)(2,1)}), bf16[1,3072,768]{2,1,0:T(8,128)(2,1)}) %all-gather.24.cloned.1.call-update) | async-done | bytes 4718608 | tf_op jit(solution)/shard_map/all_gather | solution.py:196
  308.7 6.0 fusion.115
  315.1 66.2 %all-gather.26.cloned.1.call-done = bf16[1,768,2304]{2,1,0:T(8,128)(2,1)} async-done(((bf16[1,48,2304]{2,1,0:T(8,128)(2,1)}), bf16[1,768,2304]{2,1,0:T(8,128)(2,1)}) %all-gather.26.cloned.1.call-update) | async-done | bytes 3538960 | tf_op jit(solution)/shard_map/all_gather | solution.py:193
  381.2 5.5 fusion.33
  386.7 2.8 copy.69
  389.6 2.1 fusion.1
  391.7 2.6 exponential_reduce_fusion
  394.3 1.9 copy-done.1
  396.2 3.4 convolution_convert_fusion.10
  399.6 39.0 %all-gather.28.cloned.1.call-done = bf16[1,768,768]{2,1,0:T(8,128)(2,1)} async-done(((bf16[1,48,768]{2,1,0:T(8,128)(2,1)}), bf16[1,768,768]{2,1,0:T(8,128)(2,1)}) %all-gather.28.cloned.1.call-update) | async-done | bytes 1179664 | tf_op jit(solution)/shard_map/all_gather | solution.py:194
  438.6 2.8 fusion.116
  442.9 78.4 %all-gather.30.cloned.1.call-done = bf16[1,768,3072]{2,1,0:T(8,128)(2,1)} async-done(((bf16[1,48,3072]{2,1,0:T(8,128)(2,1)}), bf16[1,768,3072]{2,1,0:T(8,128)(2,1)}) %all-gather.30.cloned.1.call-update) | async-done | bytes 4718608 | tf_op jit(solution)/shard_map/all_gather | solution.py:195
  521.4 20.8 %multiply_convert_fusion.2 = (bf16[512,3072]{1,0:T(8,128)(2,1)}, f32[512,3072]{1,0:T(8,128)}, f32[512,3072]{1,0:T(8,128)}) fusion(f32[3072]{0:T(1024)S(1)} %bitcast.255, bf16[1,768,3072]{2,1,0:T(8,128)(2,1)} %all-gather.30.cloned.1.call-done, f32[512,768]{1,0:T(8,128)} %copy-done.9, f32[768]{0:T(1024)S(1)} %get-tuple-element.36, ...), kind=kOutput, calls=%fused_computation.20 | convolution fusion | flops 2521694208 | bytes 22042624 | tf_op jit(solution)/shard_map/dot_general | solution.py:131
  542.2 61.7 %all-gather.32.cloned.1.call-done = bf16[1,3072,768]{2,1,0:T(8,128)(2,1)} async-done(((bf16[1,192,768]{2,1,0:T(8,128)(2,1)}), bf16[1,3072,768]{2,1,0:T(8,128)(2,1)}) %all-gather.32.cloned.1.call-update) | async-done | bytes 4718608 | tf_op jit(solution)/shard_map/all_gather | solution.py:196
  603.8 6.5 fusion.117
  612.1 1.7 fusion.103
  614.7 10.3 fusion.118
  625.0 5.7 multiply_reduce_fusion.3
  637.3 7.3 convolution_bitcast_fusion.1
  644.7 9.6 multiply_reduce_fusion.1
  654.3 7.4 multiply_convert_fusion.1
  661.7 2.0 multiply_bitcast_fusion.2
  666.7 4.1 convolution_convert_fusion.4
  670.8 6.0 multiply_reduce_fusion.4
  678.3 9.6 fusion.119
  687.9 7.2 multiply_reduce_fusion.5
  698.7 1.7 convolution_convert_fusion.8
  701.9 11.3 multiply_reduce_fusion
  714.7 7.1 multiply_convert_fusion
  721.7 2.0 multiply_bitcast_fusion
  724.9 3.4 convolution_bitcast_fusion
  730.7 2.0 fusion.34
  732.7 4.0 copy.90
  738.1 1.8 convolution_convert_fusion.6
  740.0 1.8 convolution_convert_fusion.7
  741.9 6.5 convolution_convert_fusion.2
  749.9 6.4 convolution_convert_fusion.3
  757.5 6.7 convolution_convert_fusion
  765.3 6.7 convolution_convert_fusion.1
  772.3 38.2 %reduce-scatter.27.cloned.1.call-done = bf16[48,2304]{1,0:T(8,128)(2,1)} async-done(((bf16[768,2304]{1,0:T(8,128)(2,1)}), bf16[48,2304]{1,0:T(8,128)(2,1)}) %reduce-scatter.27.cloned.1.call-update) | async-done | bytes 221200
  810.4 2.0 copy.93
  812.4 136.5 %reduce-scatter.25.cloned.1.call-done = bf16[48,2304]{1,0:T(8,128)(2,1)} async-done(((bf16[768,2304]{1,0:T(8,128)(2,1)}), bf16[48,2304]{1,0:T(8,128)(2,1)}) %reduce-scatter.25.cloned.1.call-update) | async-done | bytes 221200
  948.9 2.0 copy.91
  950.9 126.3 %reduce-scatter.15.cloned.1.call-done = bf16[48,768]{1,0:T(8,128)(2,1)} async-done(((bf16[768,768]{1,0:T(8,128)(2,1)}), bf16[48,768]{1,0:T(8,128)(2,1)}) %reduce-scatter.15.cloned.1.call-update) | async-done | bytes 73744 | tf_op jit(solution)/shard_map/reduce_scatter | solution.py:219
  1077.2 127.8 %reduce-scatter.13.cloned.1.call-done = bf16[48,768]{1,0:T(8,128)(2,1)} async-done(((bf16[768,768]{1,0:T(8,128)(2,1)}), bf16[48,768]{1,0:T(8,128)(2,1)}) %reduce-scatter.13.cloned.1.call-update) | async-done | bytes 73744 | tf_op jit(solution)/shard_map/reduce_scatter | solution.py:219
  1204.9 141.1 %reduce-scatter.19.cloned.1.call-done = bf16[48,3072]{1,0:T(8,128)(2,1)} async-done(((bf16[768,3072]{1,0:T(8,128)(2,1)}), bf16[48,3072]{1,0:T(8,128)(2,1)}) %reduce-scatter.19.cloned.1.call-update) | async-done | bytes 294928 | tf_op jit(solution)/shard_map/reduce_scatter | solution.py:222
  1346.0 142.7 %reduce-scatter.17.cloned.1.call-done = bf16[48,3072]{1,0:T(8,128)(2,1)} async-done(((bf16[768,3072]{1,0:T(8,128)(2,1)}), bf16[48,3072]{1,0:T(8,128)(2,1)}) %reduce-scatter.17.cloned.1.call-update) | async-done | bytes 294928 | tf_op jit(solution)/shard_map/reduce_scatter | solution.py:222
  1488.7 141.4 %reduce-scatter.23.cloned.1.call-done = bf16[192,768]{1,0:T(8,128)(2,1)} async-done(((bf16[3072,768]{1,0:T(8,128)(2,1)}), bf16[192,768]{1,0:T(8,128)(2,1)}) %reduce-scatter.23.cloned.1.call-update) | async-done | bytes 294928 | tf_op jit(solution)/shard_map/reduce_scatter | solution.py:225
  1630.1 142.5 %reduce-scatter.21.cloned.1.call-done = bf16[192,768]{1,0:T(8,128)(2,1)} async-done(((bf16[3072,768]{1,0:T(8,128)(2,1)}), bf16[192,768]{1,0:T(8,128)(2,1)}) %reduce-scatter.21.cloned.1.call-update) | async-done | bytes 294928 | tf_op jit(solution)/shard_map/reduce_scatter | solution.py:225
  1777.6 74.8 %all-reduce.2 = (bf16[9216]{0:T(1024)(128)(2,1)S(1)}, bf16[9216]{0:T(1024)(128)(2,1)S(1)}) all-reduce(bf16[9216]{0:T(1024)(128)(2,1)S(1)} %constant_dynamic-update-slice_fusion.1, bf16[9216]{0:T(1024)(128)(2,1)S(1)} %constant_dynamic-update-slice_fusion), channel_id=19, replica_groups=mesh['rep'=2,'fsdp'=16] {'fsdp'}, use_global_device_ids=true, to_apply=%region_57.58.clone | all-reduce | flops 18432 | bytes 73728
  1852.6 2.5 all-reduce.3
  1855.7 5.9 add_add_fusion.8
  (307 shorter events, 53.3 us)
Async XLA Ops:
  7.2 78.4 %all-gather.18.cloned.1.call-start = ((), (), s32[]{:S(2)}) async-start(), calls=%async_computation.14 | async-start | bytes 3760128 | tf_op jit(solution)/shard_map/all_gather | solution.py:193
  9.4 134.2 %all-gather.20.cloned.1.call-start = ((), (), s32[]{:S(2)}) async-start(), calls=%async_computation.15 | async-start | bytes 1253376 | tf_op jit(solution)/shard_map/all_gather | solution.py:194
  11.1 215.2 %all-gather.22.cloned.1.call-start = ((), (), s32[]{:S(2)}) async-start(), calls=%async_computation.16 | async-start | bytes 5013504 | tf_op jit(solution)/shard_map/all_gather | solution.py:195
  11.3 48.2 %copy-start.70 = (s32[4]{0:T(128)S(1)}, s32[4]{0:T(128)}, u32[]{:S(2)}) copy-start(s32[4]{0:T(128)} %param.9) | copy-start | bytes 52
  11.3 74.3 %copy-start.74 = (bf16[512,768]{1,0:T(8,128)(2,1)S(1)}, bf16[512,768]{1,0:T(8,128)(2,1)}, u32[]{:S(2)}) copy-start(bf16[512,768]{1,0:T(8,128)(2,1)} %param.8) | copy-start | bytes 2359300
  12.2 296.5 %all-gather.24.cloned.1.call-start = ((), (), s32[]{:S(2)}) async-start(), calls=%async_computation.17 | async-start | bytes 5013504 | tf_op jit(solution)/shard_map/all_gather | solution.py:196
  13.2 368.1 %all-gather.26.cloned.1.call-start = ((), (), s32[]{:S(2)}) async-start(), calls=%async_computation.18 | async-start | bytes 3760128 | tf_op jit(solution)/shard_map/all_gather | solution.py:193
  13.8 424.8 %all-gather.28.cloned.1.call-start = ((), (), s32[]{:S(2)}) async-start(), calls=%async_computation.19 | async-start | bytes 1253376 | tf_op jit(solution)/shard_map/all_gather | solution.py:194
  14.3 507.0 %all-gather.30.cloned.1.call-start = ((), (), s32[]{:S(2)}) async-start(), calls=%async_computation.20 | async-start | bytes 5013504 | tf_op jit(solution)/shard_map/all_gather | solution.py:195
  15.1 588.7 %all-gather.32.cloned.1.call-start = ((), (), s32[]{:S(2)}) async-start(), calls=%async_computation.21 | async-start | bytes 5013504 | tf_op jit(solution)/shard_map/all_gather | solution.py:196
  15.8 794.6 %reduce-scatter.27.cloned.1.call-start = ((), (), s32[]{:S(2)}) async-start(), calls=%async_computation.23 | async-start | bytes 3760128
  59.4 249.3 %copy-start.60 = (f32[768]{0:T(1024)}, f32[768]{0:T(1024)S(1)}, u32[]{:S(2)}) copy-start(f32[768]{0:T(1024)S(1)} %get-tuple-element.44) | copy-start | bytes 9220
  59.4 544.4 %copy-start.62 = (f32[768]{0:T(1024)}, f32[768]{0:T(1024)S(1)}, u32[]{:S(2)}) copy-start(f32[768]{0:T(1024)S(1)} %get-tuple-element.36) | copy-start | bytes 9220
  59.5 571.2 %copy-start.43 = (f32[768]{0:T(1024)}, f32[768]{0:T(1024)S(1)}, u32[]{:S(2)}) copy-start(f32[768]{0:T(1024)S(1)} %get-tuple-element.37) | copy-start | bytes 9220
  59.5 635.7 %copy-start.41 = (f32[768]{0:T(1024)}, f32[768]{0:T(1024)S(1)}, u32[]{:S(2)}) copy-start(f32[768]{0:T(1024)S(1)} %get-tuple-element.45) | copy-start | bytes 9220
  146.1 162.7 %copy-start.6 = (f32[512,768]{1,0:T(8,128)}, f32[512,768]{1,0:T(8,128)S(1)}, u32[]{:S(2)}) copy-start(f32[512,768]{1,0:T(8,128)S(1)} %get-tuple-element.107) | copy-start | bytes 4718596
  146.4 100.1 %copy-start.39 = (f32[512]{0:T(512)}, f32[512]{0:T(512)S(1)}, u32[]{:S(2)}) copy-start(f32[512]{0:T(512)S(1)} %multiply_reduce_fusion.13) | copy-start | bytes 6148
  146.4 548.8 %copy-start.47 = (f32[512]{0:T(512)}, f32[512]{0:T(512)S(1)}, u32[]{:S(2)}) copy-start(f32[512]{0:T(512)S(1)} %fusion.76) | copy-start | bytes 6148
  314.7 66.5 %copy-start.12 = (f32[512,768]{1,0:T(8,128)}, f32[512,768]{1,0:T(8,128)S(1)}, u32[]{:S(2)}) copy-start(f32[512,768]{1,0:T(8,128)S(1)} %get-tuple-element.110) | copy-start | bytes 4718596
  399.6 43.3 %copy-start.77 = (bf16[12,64,512]{2,1,0:T(8,128)(2,1)}, bf16[12,64,512]{2,1,0:T(8,128)(2,1)S(1)}, u32[]{:S(2)}) copy-start(bf16[12,64,512]{2,1,0:T(8,128)(2,1)S(1)} %convolution_convert_fusion.10) | copy-start | bytes 2359300
  441.5 189.2 %copy-start.37 = (f32[512]{0:T(512)}, f32[512]{0:T(512)S(1)}, u32[]{:S(2)}) copy-start(f32[512]{0:T(512)S(1)} %broadcast_multiply_fusion.1) | copy-start | bytes 6148
  442.9 187.8 %copy-start.49 = (f32[512]{0:T(512)}, f32[512]{0:T(512)S(1)}, u32[]{:S(2)}) copy-start(f32[512]{0:T(512)S(1)} %fusion.78) | copy-start | bytes 6148
  603.8 6.9 copy-start.16
  613.8 11.2 slice-start.6
  614.6 10.4 copy-start.21
  614.7 10.3 copy-start.10
  614.7 10.3 slice-start.7
  637.3 17.0 slice-start.3
  637.3 17.0 slice-start.4
  644.7 9.7 slice-start.5
  677.5 271.4 %reduce-scatter.25.cloned.1.call-start = ((), (), s32[]{:S(2)}) async-start(), calls=%async_computation.22 | async-start | bytes 3760128
  678.3 9.6 copy-start.23
  678.3 9.6 copy-start.7
  687.9 7.2 copy-start.80
  687.9 7.2 copy-start.40
  701.8 11.3 slice-start
  701.9 11.3 slice-start.1
  701.9 12.8 slice-start.2
  736.8 340.4 %reduce-scatter.15.cloned.1.call-start = ((), (), s32[]{:S(2)}) async-start(), calls=%async_computation.9 | async-start | bytes 1253376 | tf_op jit(solution)/shard_map/reduce_scatter | solution.py:219
  739.9 465.0 %reduce-scatter.13.cloned.1.call-start = ((), (), s32[]{:S(2)}) async-start(), calls=%async_computation.8 | async-start | bytes 1253376 | tf_op jit(solution)/shard_map/reduce_scatter | solution.py:219
  741.8 604.2 %reduce-scatter.19.cloned.1.call-start = ((), (), s32[]{:S(2)}) async-start(), calls=%async_computation.11 | async-start | bytes 5013504 | tf_op jit(solution)/shard_map/reduce_scatter | solution.py:222
  748.5 740.2 %reduce-scatter.17.cloned.1.call-start = ((), (), s32[]{:S(2)}) async-start(), calls=%async_computation.10 | async-start | bytes 5013504 | tf_op jit(solution)/shard_map/reduce_scatter | solution.py:222
  756.4 873.7 %reduce-scatter.23.cloned.1.call-start = ((), (), s32[]{:S(2)}) async-start(), calls=%async_computation.13 | async-start | bytes 5013504 | tf_op jit(solution)/shard_map/reduce_scatter | solution.py:225
  764.2 1008.4 %reduce-scatter.21.cloned.1.call-start = ((), (), s32[]{:S(2)}) async-start(), calls=%async_computation.12 | async-start | bytes 5013504 | tf_op jit(solution)/shard_map/reduce_scatter | solution.py:225
  772.0 1000.6 %copy-start.79 = (u32[32]{0:T(128)S(1)}, u32[32]{0:T(128)}, u32[]{:S(2)}) copy-start(u32[32]{0:T(128)} %constant.121) | copy-start | bytes 388
  772.0 1002.0 %copy-start.36 = (bf16[3,12,64]{2,1,0:T(8,128)(2,1)S(1)}, bf16[3,12,64]{2,1,0:T(8,128)(2,1)}, u32[]{:S(2)}) copy-start(bf16[3,12,64]{2,1,0:T(8,128)(2,1)} %get-tuple-element.65) | copy-start | bytes 13828
  772.0 1003.0 %copy-start.54 = (bf16[768]{0:T(1024)(128)(2,1)S(1)}, bf16[768]{0:T(1024)(128)(2,1)}, u32[]{:S(2)}) copy-start(bf16[768]{0:T(1024)(128)(2,1)} %get-tuple-element.69) | copy-start | bytes 4612
  772.0 1003.2 %copy-start.56 = (bf16[768]{0:T(1024)(128)(2,1)S(1)}, bf16[768]{0:T(1024)(128)(2,1)}, u32[]{:S(2)}) copy-start(bf16[768]{0:T(1024)(128)(2,1)} %get-tuple-element.63) | copy-start | bytes 4612
  772.0 1003.4 %copy-start.65 = (bf16[768]{0:T(1024)(128)(2,1)S(1)}, bf16[768]{0:T(1024)(128)(2,1)}, u32[]{:S(2)}) copy-start(bf16[768]{0:T(1024)(128)(2,1)} %get-tuple-element.25) | copy-start | bytes 4612
  772.1 1003.6 %copy-start.69 = (bf16[768]{0:T(1024)(128)(2,1)S(1)}, bf16[768]{0:T(1024)(128)(2,1)}, u32[]{:S(2)}) copy-start(bf16[768]{0:T(1024)(128)(2,1)} %get-tuple-element.23) | copy-start | bytes 4612
  772.1 1003.8 %copy-start.64 = (bf16[768]{0:T(1024)(128)(2,1)S(1)}, bf16[768]{0:T(1024)(128)(2,1)}, u32[]{:S(2)}) copy-start(bf16[768]{0:T(1024)(128)(2,1)} %get-tuple-element.31) | copy-start | bytes 4612
  772.1 1004.0 %copy-start.68 = (bf16[768]{0:T(1024)(128)(2,1)S(1)}, bf16[768]{0:T(1024)(128)(2,1)}, u32[]{:S(2)}) copy-start(bf16[768]{0:T(1024)(128)(2,1)} %get-tuple-element.30) | copy-start | bytes 4612
  772.1 1004.2 %copy-start.53 = (bf16[768]{0:T(1024)(128)(2,1)S(1)}, bf16[768]{0:T(1024)(128)(2,1)}, u32[]{:S(2)}) copy-start(bf16[768]{0:T(1024)(128)(2,1)} %get-tuple-element.67) | copy-start | bytes 4612
  772.1 1004.4 %copy-start.55 = (bf16[768]{0:T(1024)(128)(2,1)S(1)}, bf16[768]{0:T(1024)(128)(2,1)}, u32[]{:S(2)}) copy-start(bf16[768]{0:T(1024)(128)(2,1)} %get-tuple-element.61) | copy-start | bytes 4612
  772.1 1004.6 %copy-start.52 = (bf16[768]{0:T(1024)(128)(2,1)S(1)}, bf16[768]{0:T(1024)(128)(2,1)}, u32[]{:S(2)}) copy-start(bf16[768]{0:T(1024)(128)(2,1)} %get-tuple-element.27) | copy-start | bytes 4612
  772.1 1004.8 %copy-start.67 = (bf16[768]{0:T(1024)(128)(2,1)S(1)}, bf16[768]{0:T(1024)(128)(2,1)}, u32[]{:S(2)}) copy-start(bf16[768]{0:T(1024)(128)(2,1)} %get-tuple-element.21) | copy-start | bytes 4612
  772.1 1005.0 %copy-start.51 = (bf16[768]{0:T(1024)(128)(2,1)S(1)}, bf16[768]{0:T(1024)(128)(2,1)}, u32[]{:S(2)}) copy-start(bf16[768]{0:T(1024)(128)(2,1)} %get-tuple-element.32) | copy-start | bytes 4612
  772.1 1005.2 %copy-start.66 = (bf16[768]{0:T(1024)(128)(2,1)S(1)}, bf16[768]{0:T(1024)(128)(2,1)}, u32[]{:S(2)}) copy-start(bf16[768]{0:T(1024)(128)(2,1)} %get-tuple-element.29) | copy-start | bytes 4612
  772.1 1005.4 %copy-start.57 = (bf16[3072]{0:T(1024)(128)(2,1)S(1)}, bf16[3072]{0:T(1024)(128)(2,1)}, u32[]{:S(2)}) copy-start(bf16[3072]{0:T(1024)(128)(2,1)} %get-tuple-element.125) | copy-start | bytes 18436
  772.2 1005.4 %copy-start.58 = (bf16[3072]{0:T(1024)(128)(2,1)S(1)}, bf16[3072]{0:T(1024)(128)(2,1)}, u32[]{:S(2)}) copy-start(bf16[3072]{0:T(1024)(128)(2,1)} %get-tuple-element.127) | copy-start | bytes 18436
  772.2 1083.5 %copy-start.5 = (f32[512,768]{1,0:T(8,128)S(1)}, f32[512,768]{1,0:T(8,128)}, u32[]{:S(2)}) copy-start(f32[512,768]{1,0:T(8,128)} %copy-done.4) | copy-start | bytes 4718596
  772.2 1083.5 %copy-start.46 = (f32[512]{0:T(512)S(1)}, f32[512]{0:T(512)}, u32[]{:S(2)}) copy-start(f32[512]{0:T(512)} %copy-done.45) | copy-start | bytes 6148
  772.2 1089.4 %all-reduce.7.cloned.1.call-start = ((), (), s32[]{:S(2)}) async-start(), calls=%async_computation.24 | async-start | bytes 5013504 | tf_op jit(solution)/shard_map/psum | solution.py:233
  1861.6 6.4 copy-start.30
  (42 other events, 115.2 us)
Sparse Core Ops, SparseCore 0:
  11.4 74.1 all-gather.17
  88.9 54.6 all-gather.19
  147.0 79.3 all-gather.21
  229.6 79.0 all-gather.23
  311.3 69.8 all-gather.25
  383.9 54.6 all-gather.27
  442.0 79.3 all-gather.29
  524.7 79.0 all-gather.31
  677.6 132.7 reduce-scatter.26
  815.4 133.4 reduce-scatter.24
  954.2 122.8 reduce-scatter.14
  1082.3 122.5 reduce-scatter.12
  1210.1 135.8 reduce-scatter.18
  1351.9 136.7 reduce-scatter.16
  1493.7 136.3 reduce-scatter.22
  1636.0 136.6 reduce-scatter.20
  1775.9 21.4 all-reduce.6
where the time goes:
time: 1880 us
  waiting for transfers between devices  1450 us (77%)
  matrix products  203 us (11%)
  blocking collectives  121 us (6%)
  local copies, waits for them, and re-layouts  46 us (2%)
  other arithmetic  38.7 us (2%)
    reduce_scatter x2, waiting for transfers between devices, shards(): lax.psum_scatter(term_down.astype(jnp.bfloat16), 'fsdp', scatter_dimensio...  284 us
    reduce_scatter x2, waiting for transfers between devices, shards(): lax.psum_scatter(term_up.astype(jnp.bfloat16), 'fsdp', scatter_dimension=...  284 us
    reduce_scatter x2, waiting for transfers between devices, shards(): lax.psum_scatter(term_out.astype(jnp.bfloat16), 'fsdp', scatter_dimension...  254 us
    unnamed x19, waiting for transfers between devices  177 us
    all_gather x2, waiting for transfers between devices, shards(): lax.all_gather(up_weight[level_idx].astype(jnp.bfloat16), 'fsdp', axis=0,...  158 us
    all_gather x2, waiting for transfers between devices, shards(): lax.all_gather(down_weight[level_idx].astype(jnp.bfloat16), 'fsdp', axis=...  124 us
    all_gather x2, waiting for transfers between devices, shards(): lax.all_gather(qkv_weight[level_idx].astype(jnp.bfloat16), 'fsdp', axis=0...  91.8 us
    all_gather x2, waiting for transfers between devices, shards(): lax.all_gather(out_weight[level_idx].astype(jnp.bfloat16), 'fsdp', axis=0...  77.4 us
  transfers between devices with their start and end apart: 17, of which 16 were waited for; matrix products, arithmetic and copies ran while one was open for 10% of the time, Pallas kernels for 0%

commit v1 on v0

--- a/solution.py
+++ b/solution.py
@@ -190,7 +190,17 @@
     kept_saved = []
     for level_idx in range(LAYERS):
         weights = (
-            lax.all_gather(qkv_weight[level_idx].astype(jnp.bfloat16), "fsdp", axis=0, tiled=True),
+            jnp.concatenate(
+                jax.lax.all_to_all(
+                    jnp.stack(
+                        [qkv_weight[level_idx].astype(jnp.bfloat16)] * jax.lax.axis_size("fsdp"), 0
+                    ),
+                    "fsdp",
+                    0,
+                    0,
+                ),
+                0,
+            ),
             lax.all_gather(out_weight[level_idx].astype(jnp.bfloat16), "fsdp", axis=0, tiled=True),
             lax.all_gather(up_weight[level_idx].astype(jnp.bfloat16), "fsdp", axis=0, tiled=True),
             lax.all_gather(down_weight[level_idx].astype(jnp.bfloat16), "fsdp", axis=0, tiled=True),

time: 1880 us -> 1840 us (0.979)
  waiting for transfers between devices: 1450 us -> 1320 us
  blocking collectives: 121 us -> 175 us
  starting transfers between devices: 0.94 us -> 31.9 us
    all_gather x2, waiting for transfers between devices: 91.8 us -> 6.36 us  [shards(): lax.all_gather(qkv_weight[level_idx].astype(jnp.bfloat16), 'fsdp', axis=0...]
    all_gather x1, blocking collectives: 43.3 us -> 96.3 us  [shards(): vector_all = lax.all_gather(vectors, 'fsdp', axis=1, tiled=True)]
    all_gather x2, waiting for transfers between devices: 77.4 us -> 31.9 us  [shards(): lax.all_gather(out_weight[level_idx].astype(jnp.bfloat16), 'fsdp', axis=0...]
    all_to_all x0 -> x2, starting transfers between devices: none -> 30.9 us  [shards(): jax.lax.all_to_all(jnp.stack([qkv_weight[level_idx].astype(jnp.bfloat16)]...]
  transfers between devices with their start and end apart: 17 -> 19, of which waited for: 16 -> 15; matrix products, arithmetic and copies ran while one was open for 10% -> 14% of each run, Pallas kernels for 0% -> 0%
where the time goes in v1:
time: 1840 us
  waiting for transfers between devices  1320 us (72%)
  matrix products  201 us (11%)
  blocking collectives  175 us (10%)
  local copies, waits for them, and re-layouts  53 us (3%)
  other arithmetic  38.9 us (2%)
  starting transfers between devices  31.9 us (2%)
    reduce_scatter x2, waiting for transfers between devices, shards(): lax.psum_scatter(term_up.astype(jnp.bfloat16), 'fsdp', scatter_dimension=...  284 us
    reduce_scatter x2, waiting for transfers between devices, shards(): lax.psum_scatter(term_down.astype(jnp.bfloat16), 'fsdp', scatter_dimensio...  284 us
    reduce_scatter x2, waiting for transfers between devices, shards(): lax.psum_scatter(term_out.astype(jnp.bfloat16), 'fsdp', scatter_dimension...  254 us
    unnamed x19, waiting for transfers between devices  177 us
    all_gather x2, waiting for transfers between devices, shards(): lax.all_gather(up_weight[level_idx].astype(jnp.bfloat16), 'fsdp', axis=0,...  148 us
    all_gather x2, waiting for transfers between devices, shards(): lax.all_gather(down_weight[level_idx].astype(jnp.bfloat16), 'fsdp', axis=...  127 us
    all_gather x1, blocking collectives, shards(): vector_all = lax.all_gather(vectors, 'fsdp', axis=1, tiled=True)  96.3 us
    unnamed x1, blocking collectives  76 us
  transfers between devices with their start and end apart: 19, of which 15 were waited for; matrix products, arithmetic and copies ran while one was open for 14% of the time, Pallas kernels for 0%

profile of v1, /device:TPU:0, one launch (start us, length us, event | category | flops | bytes accessed | tf_op | source)
XLA Modules:
  0.0 1835.6 jit_solution(15300046695870384535)
XLA Ops:
  14.8 2.0 stack.137
  16.9 8.5 all-to-all-start
  26.1 96.3 %all-gather.8 = f32[16,576,2]{1,2,0:T(2,128)S(1)} all-gather(f32[1,576,2]{1,2,0:T(2,128)S(1)} %bitcast.261), channel_id=1, replica_groups=mesh['rep'=2,'fsdp'=16] {'fsdp'}, dimensions={0}, use_global_device_ids=true | all-gather | bytes 78336 | tf_op jit(solution)/shard_map/all_gather | solution.py:187
  123.7 2.0 stack.139
  125.7 22.4 %all-to-all-start.1 = ((bf16[16,48,2304]{2,1,0:T(8,128)(2,1)}), bf16[16,48,2304]{2,1,0:T(8,128)(2,1)}, u32[]{:S(2)}, u32[]{:S(2)}) async-start(bf16[16,48,2304]{2,1,0:T(8,128)(2,1)} %stack.139), calls=%async_computation.1 | async-start | bytes 7077888 | tf_op jit(solution)/shard_map/all_to_all | solution.py:194
  148.2 5.4 fusion.32
  153.6 3.0 copy.67
  156.7 2.1 fusion
  158.8 2.6 exponential_reduce_fusion.1
  161.4 2.0 copy-done
  163.9 3.9 convolution_convert_fusion.11
  167.9 2.5 fusion.112
  170.7 69.9 %all-gather.20.cloned.1.call-done = bf16[1,768,3072]{2,1,0:T(8,128)(2,1)} async-done(((bf16[1,48,3072]{2,1,0:T(8,128)(2,1)}), bf16[1,768,3072]{2,1,0:T(8,128)(2,1)}) %all-gather.20.cloned.1.call-update) | async-done | bytes 4718608 | tf_op jit(solution)/shard_map/all_gather | solution.py:205
  240.6 20.1 %multiply_convert_fusion.3 = (bf16[512,3072]{1,0:T(8,128)(2,1)}, f32[512,3072]{1,0:T(8,128)}, f32[512,3072]{1,0:T(8,128)}) fusion(f32[3072]{0:T(1024)S(1)} %bitcast.257, bf16[1,768,3072]{2,1,0:T(8,128)(2,1)} %all-gather.20.cloned.1.call-done, f32[512,768]{1,0:T(8,128)S(1)} %get-tuple-element.107, f32[768]{0:T(1024)S(1)} %get-tuple-element.44, ...), kind=kOutput, calls=%fused_computation.33 | convolution fusion | flops 2521694208 | bytes 22042624 | tf_op jit(solution)/shard_map/dot_general | solution.py:131
  260.7 65.0 %all-gather.22.cloned.1.call-done = bf16[1,3072,768]{2,1,0:T(8,128)(2,1)} async-done(((bf16[1,192,768]{2,1,0:T(8,128)(2,1)}), bf16[1,3072,768]{2,1,0:T(8,128)(2,1)}) %all-gather.22.cloned.1.call-update) | async-done | bytes 4718608 | tf_op jit(solution)/shard_map/all_gather | solution.py:206
  325.7 6.0 fusion.113
  332.8 5.5 fusion.33
  338.4 2.8 copy.69
  341.2 2.1 fusion.1
  343.3 2.6 exponential_reduce_fusion
  345.9 1.9 copy-done.1
  347.8 3.4 convolution_convert_fusion.10
  351.2 31.9 %all-gather.24.cloned.1.call-done = bf16[1,768,768]{2,1,0:T(8,128)(2,1)} async-done(((bf16[1,48,768]{2,1,0:T(8,128)(2,1)}), bf16[1,768,768]{2,1,0:T(8,128)(2,1)}) %all-gather.24.cloned.1.call-update) | async-done | bytes 1179664 | tf_op jit(solution)/shard_map/all_gather | solution.py:204
  383.1 2.8 fusion.114
  387.4 78.2 %all-gather.26.cloned.1.call-done = bf16[1,768,3072]{2,1,0:T(8,128)(2,1)} async-done(((bf16[1,48,3072]{2,1,0:T(8,128)(2,1)}), bf16[1,768,3072]{2,1,0:T(8,128)(2,1)}) %all-gather.26.cloned.1.call-update) | async-done | bytes 4718608 | tf_op jit(solution)/shard_map/all_gather | solution.py:205
  465.7 20.8 %multiply_convert_fusion.2 = (bf16[512,3072]{1,0:T(8,128)(2,1)}, f32[512,3072]{1,0:T(8,128)}, f32[512,3072]{1,0:T(8,128)}) fusion(f32[3072]{0:T(1024)S(1)} %bitcast.259, bf16[1,768,3072]{2,1,0:T(8,128)(2,1)} %all-gather.26.cloned.1.call-done, f32[512,768]{1,0:T(8,128)} %copy-done.9, f32[768]{0:T(1024)S(1)} %get-tuple-element.36, ...), kind=kOutput, calls=%fused_computation.20 | convolution fusion | flops 2521694208 | bytes 22042624 | tf_op jit(solution)/shard_map/dot_general | solution.py:131
  486.5 61.6 %all-gather.28.cloned.1.call-done = bf16[1,3072,768]{2,1,0:T(8,128)(2,1)} async-done(((bf16[1,192,768]{2,1,0:T(8,128)(2,1)}), bf16[1,3072,768]{2,1,0:T(8,128)(2,1)}) %all-gather.28.cloned.1.call-update) | async-done | bytes 4718608 | tf_op jit(solution)/shard_map/all_gather | solution.py:206
  548.1 6.5 fusion.115
  559.0 10.4 fusion.116
  569.5 5.7 multiply_reduce_fusion.3
  581.9 11.2 multiply_reduce_fusion.1
  594.5 7.5 multiply_convert_fusion.1
  602.0 2.0 multiply_bitcast_fusion.2
  605.2 3.2 convolution_bitcast_fusion.1
  610.2 4.2 convolution_convert_fusion.4
  614.4 6.4 all-gather.30.cloned.1.call-done
  620.7 6.0 multiply_reduce_fusion.4
  628.2 9.6 fusion.117
  637.8 7.2 multiply_reduce_fusion.5
  651.8 11.3 multiply_reduce_fusion
  664.6 7.1 multiply_convert_fusion
  671.7 2.0 multiply_bitcast_fusion
  674.8 3.4 convolution_bitcast_fusion
  680.6 2.0 fusion.34
  682.6 4.0 copy.90
  689.9 1.8 convolution_convert_fusion.7
  691.8 6.4 convolution_convert_fusion.2
  699.7 6.5 convolution_convert_fusion.3
  707.4 6.8 convolution_convert_fusion
  715.3 6.7 convolution_convert_fusion.1
  722.8 37.7 %reduce-scatter.27.cloned.1.call-done = bf16[48,2304]{1,0:T(8,128)(2,1)} async-done(((bf16[768,2304]{1,0:T(8,128)(2,1)}), bf16[48,2304]{1,0:T(8,128)(2,1)}) %reduce-scatter.27.cloned.1.call-update) | async-done | bytes 221200
  760.5 2.0 copy.93
  762.5 136.8 %reduce-scatter.25.cloned.1.call-done = bf16[48,2304]{1,0:T(8,128)(2,1)} async-done(((bf16[768,2304]{1,0:T(8,128)(2,1)}), bf16[48,2304]{1,0:T(8,128)(2,1)}) %reduce-scatter.25.cloned.1.call-update) | async-done | bytes 221200
  899.3 2.1 copy.91
  901.3 126.0 %reduce-scatter.15.cloned.1.call-done = bf16[48,768]{1,0:T(8,128)(2,1)} async-done(((bf16[768,768]{1,0:T(8,128)(2,1)}), bf16[48,768]{1,0:T(8,128)(2,1)}) %reduce-scatter.15.cloned.1.call-update) | async-done | bytes 73744 | tf_op jit(solution)/shard_map/reduce_scatter | solution.py:229
  1027.3 128.0 %reduce-scatter.13.cloned.1.call-done = bf16[48,768]{1,0:T(8,128)(2,1)} async-done(((bf16[768,768]{1,0:T(8,128)(2,1)}), bf16[48,768]{1,0:T(8,128)(2,1)}) %reduce-scatter.13.cloned.1.call-update) | async-done | bytes 73744 | tf_op jit(solution)/shard_map/reduce_scatter | solution.py:229
  1155.3 141.4 %reduce-scatter.19.cloned.1.call-done = bf16[48,3072]{1,0:T(8,128)(2,1)} async-done(((bf16[768,3072]{1,0:T(8,128)(2,1)}), bf16[48,3072]{1,0:T(8,128)(2,1)}) %reduce-scatter.19.cloned.1.call-update) | async-done | bytes 294928 | tf_op jit(solution)/shard_map/reduce_scatter | solution.py:232
  1296.7 142.7 %reduce-scatter.17.cloned.1.call-done = bf16[48,3072]{1,0:T(8,128)(2,1)} async-done(((bf16[768,3072]{1,0:T(8,128)(2,1)}), bf16[48,3072]{1,0:T(8,128)(2,1)}) %reduce-scatter.17.cloned.1.call-update) | async-done | bytes 294928 | tf_op jit(solution)/shard_map/reduce_scatter | solution.py:232
  1439.4 141.5 %reduce-scatter.23.cloned.1.call-done = bf16[192,768]{1,0:T(8,128)(2,1)} async-done(((bf16[3072,768]{1,0:T(8,128)(2,1)}), bf16[192,768]{1,0:T(8,128)(2,1)}) %reduce-scatter.23.cloned.1.call-update) | async-done | bytes 294928 | tf_op jit(solution)/shard_map/reduce_scatter | solution.py:235
  1580.9 142.3 %reduce-scatter.21.cloned.1.call-done = bf16[192,768]{1,0:T(8,128)(2,1)} async-done(((bf16[3072,768]{1,0:T(8,128)(2,1)}), bf16[192,768]{1,0:T(8,128)(2,1)}) %reduce-scatter.21.cloned.1.call-update) | async-done | bytes 294928 | tf_op jit(solution)/shard_map/reduce_scatter | solution.py:235
  1728.2 76.0 %all-reduce.2 = (bf16[9216]{0:T(1024)(128)(2,1)S(1)}, bf16[9216]{0:T(1024)(128)(2,1)S(1)}) all-reduce(bf16[9216]{0:T(1024)(128)(2,1)S(1)} %constant_dynamic-update-slice_fusion.1, bf16[9216]{0:T(1024)(128)(2,1)S(1)} %constant_dynamic-update-slice_fusion), channel_id=19, replica_groups=mesh['rep'=2,'fsdp'=16] {'fsdp'}, use_global_device_ids=true, to_apply=%region_57.58.clone | all-reduce | flops 18432 | bytes 73728
  1804.4 2.5 all-reduce.3
  1807.5 6.1 add_add_fusion.8
  1813.6 7.5 all-reduce.7.cloned.1.call-done
  (316 shorter events, 61.8 us)
Async XLA Ops:
  7.2 160.7 %all-gather.18.cloned.1.call-start = ((), (), s32[]{:S(2)}) async-start(), calls=%async_computation.16 | async-start | bytes 1253376 | tf_op jit(solution)/shard_map/all_gather | solution.py:204
  9.0 231.6 %all-gather.20.cloned.1.call-start = ((), (), s32[]{:S(2)}) async-start(), calls=%async_computation.17 | async-start | bytes 5013504 | tf_op jit(solution)/shard_map/all_gather | solution.py:205
  11.3 314.3 %all-gather.22.cloned.1.call-start = ((), (), s32[]{:S(2)}) async-start(), calls=%async_computation.18 | async-start | bytes 5013504 | tf_op jit(solution)/shard_map/all_gather | solution.py:206
  12.3 370.8 %all-gather.24.cloned.1.call-start = ((), (), s32[]{:S(2)}) async-start(), calls=%async_computation.19 | async-start | bytes 1253376 | tf_op jit(solution)/shard_map/all_gather | solution.py:204
  12.9 452.8 %all-gather.26.cloned.1.call-start = ((), (), s32[]{:S(2)}) async-start(), calls=%async_computation.20 | async-start | bytes 5013504 | tf_op jit(solution)/shard_map/all_gather | solution.py:205
  13.5 534.5 %all-gather.28.cloned.1.call-start = ((), (), s32[]{:S(2)}) async-start(), calls=%async_computation.21 | async-start | bytes 5013504 | tf_op jit(solution)/shard_map/all_gather | solution.py:206
  16.9 9.3 copy-start.61
  16.9 106.4 %copy-start.72 = (s32[4]{0:T(128)S(1)}, s32[4]{0:T(128)}, u32[]{:S(2)}) copy-start(s32[4]{0:T(128)} %param.9) | copy-start | bytes 52
  16.9 106.8 %copy-start.20 = (bf16[1,48,2304]{2,1,0:T(8,128)(2,1)S(1)}, bf16[1,48,2304]{2,1,0:T(8,128)(2,1)}, u32[]{:S(2)}) copy-start(bf16[1,48,2304]{2,1,0:T(8,128)(2,1)} %get-tuple-element.89) | copy-start | bytes 663556
  16.9 106.8 %all-to-all-start = ((bf16[16,48,2304]{2,1,0:T(8,128)(2,1)}), bf16[16,48,2304]{2,1,0:T(8,128)(2,1)}, u32[]{:S(2)}, u32[]{:S(2)}) async-start(bf16[16,48,2304]{2,1,0:T(8,128)(2,1)} %stack.137), calls=%async_computation | async-start | bytes 7077888 | tf_op jit(solution)/shard_map/all_to_all | solution.py:194
  25.4 595.4 %all-gather.30.cloned.1.call-start = ((), (), s32[]{:S(2)}) async-start(), calls=%async_computation.22 | async-start | bytes 3760128 | tf_op jit(solution)/shard_map/all_gather | solution.py:216
  123.2 202.4 %copy-start.62 = (f32[768]{0:T(1024)}, f32[768]{0:T(1024)S(1)}, u32[]{:S(2)}) copy-start(f32[768]{0:T(1024)S(1)} %get-tuple-element.44) | copy-start | bytes 9220
  123.2 424.8 %copy-start.64 = (f32[768]{0:T(1024)}, f32[768]{0:T(1024)S(1)}, u32[]{:S(2)}) copy-start(f32[768]{0:T(1024)S(1)} %get-tuple-element.36) | copy-start | bytes 9220
  123.2 452.0 %copy-start.44 = (f32[768]{0:T(1024)}, f32[768]{0:T(1024)S(1)}, u32[]{:S(2)}) copy-start(f32[768]{0:T(1024)S(1)} %get-tuple-element.37) | copy-start | bytes 9220
  123.2 521.8 %copy-start.42 = (f32[768]{0:T(1024)}, f32[768]{0:T(1024)S(1)}, u32[]{:S(2)}) copy-start(f32[768]{0:T(1024)S(1)} %get-tuple-element.45) | copy-start | bytes 9220
  125.7 22.5 %copy-start.76 = (bf16[512,768]{1,0:T(8,128)(2,1)S(1)}, bf16[512,768]{1,0:T(8,128)(2,1)}, u32[]{:S(2)}) copy-start(bf16[512,768]{1,0:T(8,128)(2,1)} %param.8) | copy-start | bytes 2359300
  125.7 206.3 %all-to-all-start.1 = ((bf16[16,48,2304]{2,1,0:T(8,128)(2,1)}), bf16[16,48,2304]{2,1,0:T(8,128)(2,1)}, u32[]{:S(2)}, u32[]{:S(2)}) async-start(bf16[16,48,2304]{2,1,0:T(8,128)(2,1)} %stack.139), calls=%async_computation.1 | async-start | bytes 7077888 | tf_op jit(solution)/shard_map/all_to_all | solution.py:194
  148.1 612.4 %reduce-scatter.27.cloned.1.call-start = ((), (), s32[]{:S(2)}) async-start(), calls=%async_computation.25 | async-start | bytes 3760128
  170.3 155.3 %copy-start.6 = (f32[512,768]{1,0:T(8,128)}, f32[512,768]{1,0:T(8,128)S(1)}, u32[]{:S(2)}) copy-start(f32[512,768]{1,0:T(8,128)S(1)} %get-tuple-element.107) | copy-start | bytes 4718596
  170.6 90.0 %copy-start.40 = (f32[512]{0:T(512)}, f32[512]{0:T(512)S(1)}, u32[]{:S(2)}) copy-start(f32[512]{0:T(512)S(1)} %multiply_reduce_fusion.13) | copy-start | bytes 6148
  170.7 474.4 %copy-start.49 = (f32[512]{0:T(512)}, f32[512]{0:T(512)S(1)}, u32[]{:S(2)}) copy-start(f32[512]{0:T(512)S(1)} %fusion.74) | copy-start | bytes 6148
  351.2 36.2 %copy-start.79 = (bf16[12,64,512]{2,1,0:T(8,128)(2,1)}, bf16[12,64,512]{2,1,0:T(8,128)(2,1)S(1)}, u32[]{:S(2)}) copy-start(bf16[12,64,512]{2,1,0:T(8,128)(2,1)S(1)} %convolution_convert_fusion.10) | copy-start | bytes 2359300
  385.9 189.3 %copy-start.38 = (f32[512]{0:T(512)}, f32[512]{0:T(512)S(1)}, u32[]{:S(2)}) copy-start(f32[512]{0:T(512)S(1)} %broadcast_multiply_fusion.1) | copy-start | bytes 6148
  387.4 187.8 %copy-start.51 = (f32[512]{0:T(512)}, f32[512]{0:T(512)S(1)}, u32[]{:S(2)}) copy-start(f32[512]{0:T(512)S(1)} %fusion.76) | copy-start | bytes 6148
  558.0 11.5 slice-start.6
  558.8 10.7 copy-start.22
  559.0 10.4 copy-start.10
  559.0 10.4 slice-start.7
  581.8 11.2 slice-start.3
  581.8 11.2 slice-start.4
  581.9 12.7 slice-start.5
  610.2 10.5 copy-start.15
  627.4 271.9 %reduce-scatter.25.cloned.1.call-start = ((), (), s32[]{:S(2)}) async-start(), calls=%async_computation.24 | async-start | bytes 3760128
  628.2 9.6 copy-start.24
  628.2 9.6 copy-start.7
  651.7 11.3 slice-start
  651.7 11.3 slice-start.1
  651.8 12.8 slice-start.2
  686.7 340.6 %reduce-scatter.15.cloned.1.call-start = ((), (), s32[]{:S(2)}) async-start(), calls=%async_computation.11 | async-start | bytes 1253376 | tf_op jit(solution)/shard_map/reduce_scatter | solution.py:229
  689.8 465.4 %reduce-scatter.13.cloned.1.call-start = ((), (), s32[]{:S(2)}) async-start(), calls=%async_computation.10 | async-start | bytes 1253376 | tf_op jit(solution)/shard_map/reduce_scatter | solution.py:229
  691.7 605.0 %reduce-scatter.19.cloned.1.call-start = ((), (), s32[]{:S(2)}) async-start(), calls=%async_computation.13 | async-start | bytes 5013504 | tf_op jit(solution)/shard_map/reduce_scatter | solution.py:232
  698.3 741.1 %reduce-scatter.17.cloned.1.call-start = ((), (), s32[]{:S(2)}) async-start(), calls=%async_computation.12 | async-start | bytes 5013504 | tf_op jit(solution)/shard_map/reduce_scatter | solution.py:232
  706.3 874.6 %reduce-scatter.23.cloned.1.call-start = ((), (), s32[]{:S(2)}) async-start(), calls=%async_computation.15 | async-start | bytes 5013504 | tf_op jit(solution)/shard_map/reduce_scatter | solution.py:235
  714.2 1009.0 %reduce-scatter.21.cloned.1.call-start = ((), (), s32[]{:S(2)}) async-start(), calls=%async_computation.14 | async-start | bytes 5013504 | tf_op jit(solution)/shard_map/reduce_scatter | solution.py:235
  722.0 1001.2 %copy-start.81 = (u32[32]{0:T(128)S(1)}, u32[32]{0:T(128)}, u32[]{:S(2)}) copy-start(u32[32]{0:T(128)} %constant.121) | copy-start | bytes 388
  722.0 1002.7 %copy-start.37 = (bf16[3,12,64]{2,1,0:T(8,128)(2,1)S(1)}, bf16[3,12,64]{2,1,0:T(8,128)(2,1)}, u32[]{:S(2)}) copy-start(bf16[3,12,64]{2,1,0:T(8,128)(2,1)} %get-tuple-element.65) | copy-start | bytes 13828
  722.0 1003.6 %copy-start.56 = (bf16[768]{0:T(1024)(128)(2,1)S(1)}, bf16[768]{0:T(1024)(128)(2,1)}, u32[]{:S(2)}) copy-start(bf16[768]{0:T(1024)(128)(2,1)} %get-tuple-element.69) | copy-start | bytes 4612
  722.0 1003.8 %copy-start.58 = (bf16[768]{0:T(1024)(128)(2,1)S(1)}, bf16[768]{0:T(1024)(128)(2,1)}, u32[]{:S(2)}) copy-start(bf16[768]{0:T(1024)(128)(2,1)} %get-tuple-element.63) | copy-start | bytes 4612
  722.0 1004.0 %copy-start.67 = (bf16[768]{0:T(1024)(128)(2,1)S(1)}, bf16[768]{0:T(1024)(128)(2,1)}, u32[]{:S(2)}) copy-start(bf16[768]{0:T(1024)(128)(2,1)} %get-tuple-element.25) | copy-start | bytes 4612
  722.0 1004.2 %copy-start.71 = (bf16[768]{0:T(1024)(128)(2,1)S(1)}, bf16[768]{0:T(1024)(128)(2,1)}, u32[]{:S(2)}) copy-start(bf16[768]{0:T(1024)(128)(2,1)} %get-tuple-element.23) | copy-start | bytes 4612
  722.1 1004.4 %copy-start.66 = (bf16[768]{0:T(1024)(128)(2,1)S(1)}, bf16[768]{0:T(1024)(128)(2,1)}, u32[]{:S(2)}) copy-start(bf16[768]{0:T(1024)(128)(2,1)} %get-tuple-element.31) | copy-start | bytes 4612
  722.1 1004.6 %copy-start.70 = (bf16[768]{0:T(1024)(128)(2,1)S(1)}, bf16[768]{0:T(1024)(128)(2,1)}, u32[]{:S(2)}) copy-start(bf16[768]{0:T(1024)(128)(2,1)} %get-tuple-element.30) | copy-start | bytes 4612
  722.1 1004.9 %copy-start.55 = (bf16[768]{0:T(1024)(128)(2,1)S(1)}, bf16[768]{0:T(1024)(128)(2,1)}, u32[]{:S(2)}) copy-start(bf16[768]{0:T(1024)(128)(2,1)} %get-tuple-element.67) | copy-start | bytes 4612
  722.1 1005.1 %copy-start.57 = (bf16[768]{0:T(1024)(128)(2,1)S(1)}, bf16[768]{0:T(1024)(128)(2,1)}, u32[]{:S(2)}) copy-start(bf16[768]{0:T(1024)(128)(2,1)} %get-tuple-element.61) | copy-start | bytes 4612
  722.1 1005.3 %copy-start.54 = (bf16[768]{0:T(1024)(128)(2,1)S(1)}, bf16[768]{0:T(1024)(128)(2,1)}, u32[]{:S(2)}) copy-start(bf16[768]{0:T(1024)(128)(2,1)} %get-tuple-element.27) | copy-start | bytes 4612
  722.1 1005.5 %copy-start.69 = (bf16[768]{0:T(1024)(128)(2,1)S(1)}, bf16[768]{0:T(1024)(128)(2,1)}, u32[]{:S(2)}) copy-start(bf16[768]{0:T(1024)(128)(2,1)} %get-tuple-element.21) | copy-start | bytes 4612
  722.1 1005.7 %copy-start.53 = (bf16[768]{0:T(1024)(128)(2,1)S(1)}, bf16[768]{0:T(1024)(128)(2,1)}, u32[]{:S(2)}) copy-start(bf16[768]{0:T(1024)(128)(2,1)} %get-tuple-element.32) | copy-start | bytes 4612
  722.1 1005.9 %copy-start.68 = (bf16[768]{0:T(1024)(128)(2,1)S(1)}, bf16[768]{0:T(1024)(128)(2,1)}, u32[]{:S(2)}) copy-start(bf16[768]{0:T(1024)(128)(2,1)} %get-tuple-element.29) | copy-start | bytes 4612
  722.1 1006.1 %copy-start.59 = (bf16[3072]{0:T(1024)(128)(2,1)S(1)}, bf16[3072]{0:T(1024)(128)(2,1)}, u32[]{:S(2)}) copy-start(bf16[3072]{0:T(1024)(128)(2,1)} %get-tuple-element.125) | copy-start | bytes 18436
  722.1 1006.1 %copy-start.60 = (bf16[3072]{0:T(1024)(128)(2,1)S(1)}, bf16[3072]{0:T(1024)(128)(2,1)}, u32[]{:S(2)}) copy-start(bf16[3072]{0:T(1024)(128)(2,1)} %get-tuple-element.127) | copy-start | bytes 18436
  722.2 1085.3 %copy-start.5 = (f32[512,768]{1,0:T(8,128)S(1)}, f32[512,768]{1,0:T(8,128)}, u32[]{:S(2)}) copy-start(f32[512,768]{1,0:T(8,128)} %copy-done.4) | copy-start | bytes 4718596
  722.2 1085.3 %copy-start.48 = (f32[512]{0:T(512)S(1)}, f32[512]{0:T(512)}, u32[]{:S(2)}) copy-start(f32[512]{0:T(512)} %copy-done.47) | copy-start | bytes 6148
  722.2 1085.3 %all-gather.32.cloned.1.call-start = ((), (), s32[]{:S(2)}) async-start(), calls=%async_computation.23 | async-start | bytes 3760128 | tf_op jit(solution)/shard_map/all_gather | solution.py:216
  722.8 1098.4 %all-reduce.7.cloned.1.call-start = ((), (), s32[]{:S(2)}) async-start(), calls=%async_computation.26 | async-start | bytes 5013504 | tf_op jit(solution)/shard_map/psum | solution.py:243
  (46 other events, 138.0 us)
Sparse Core Ops, SparseCore 0:
  11.4 99.3 all-gather.17
  114.1 126.4 all-gather.19
  244.0 81.6 all-gather.21
  328.3 54.7 all-gather.23
  386.3 79.3 all-gather.25
  468.9 79.0 all-gather.27
  550.8 69.8 all-gather.29
  627.5 132.9 reduce-scatter.26
  765.6 133.6 reduce-scatter.24
  904.4 122.7 reduce-scatter.14
  1032.6 122.5 reduce-scatter.12
  1160.3 136.3 reduce-scatter.18
  1302.7 136.6 reduce-scatter.16
  1444.4 136.4 reduce-scatter.22
  1586.7 136.4 reduce-scatter.20
  1725.9 70.8 all-gather.31
  1800.1 21.0 all-reduce.6
